TPU v7x, 32 devices: a whole 2x2x4 slice. The times are simulated.
32 devices in a mesh: ent: 8 (over z, x), qry: 4 (over y, core).
Axes of the slice: x: 2, y: 2, z: 4, core: 2. Of those that a mesh axis runs over, the one named last changes fastest.
Arguments:
- ent_feat: bfloat16 [64, 8192], P(None, 'ent'), may hold values from -6 to 6
- query_head: int32 [16], replicated, may hold values from 0 to 8191
- query_rel: int32 [16], replicated, may hold values from 0 to 821
- query_table: bfloat16 [822, 64], replicated, may hold values from -5 to 5
- rel_table: bfloat16 [3, 822, 64], replicated, may hold values from -5 to 5
- layer_weight: bfloat16 [3, 64, 64], replicated, may hold values from -0.75 to 0.75
- layer_bias: float32 [3, 64], replicated, may hold values from -5 to 5
- norm_gain: float32 [3, 64], replicated, may hold values from 0.5 to 1.5
- norm_shift: float32 [3, 64], replicated, may hold values from -3 to 3
- reg_blocks: int32 [640, 2], P('ent'), may hold values from 0 to 63, as said below
- reg_rel: int32 [640], P('ent'), may hold values from 0 to 821
- reg_mask: int32 [640, 128, 128], P('ent'), may hold values 0 or 1
- hin_blocks: int32 [192, 2], P('ent'), may hold values from 0 to 63, as said below
- hin_rel: int32 [192], P('ent'), may hold values from 0 to 821
- hin_mask: int32 [192, 128, 128], P('ent'), may hold values 0 or 1
- hout_blocks: int32 [192, 2], P('ent'), may hold values from 0 to 63, as said below
- hout_rel: int32 [192], P('ent'), may hold values from 0 to 821
- hout_mask: int32 [192, 128, 128], P('ent'), may hold values 0 or 1
- read_weight: bfloat16 [128, 64], replicated, may hold values from -0.5 to 0.5
- read_bias: float32 [64], replicated, may hold values from -5 to 5
- read_out: float32 [64], replicated, may hold values from -0.75 to 0.75
Outputs:
- scores: float32 [16, 8192], P(None, ('ent', 'qry'))
- hub_scores: float32 [16, 128], P('qry', 'ent')
Inputs may be any that keep to these rules, and one draw needn't show every extreme that they name: `reg_blocks`: rows are grouped by 80 per index of ent. Column 0 is a block of that index's own 8 blocks; column 1 is a block of the same index's or an adjacent index's entities. `hin_blocks`: rows are grouped by 24 per index of ent. Column 0 is a hub block, below 1; column 1 is a block of that index's own entities. `hout_blocks`: rows are grouped by 24 per index of ent. Column 0 is a block of that index's own entities; column 1 is a hub block, below 1.
All inputs are finite; a program needn't handle non-finite values. No bound on the sum of `reg_mask` or of `hin_mask` or of `hout_mask` on one device may be relied on, other than what follows from the above.
Results may differ from a plain program's by a relative error of at most 0.0075.
Values may be sent and summed in bfloat16 or wider, within the bound.
No kernel may reach another device: no remote copies, remote signals or barrier semaphores. Data moves between devices by JAX's collectives and lax.ppermute only.
A program may use at most 128 MiB of HBM per device.

v0:
```python
import jax
import jax.numpy as jnp
from jax import lax
from jax.sharding import PartitionSpec as P

LAYERS = 3
HUB_DEV = 16


def padded(cells, sides, width):
    for axis, dim in sides:
        count = lax.axis_size(axis)
        ends = count - 1
        head = lax.slice_in_dim(cells, 0, width, axis=dim)
        tail = lax.slice_in_dim(cells, cells.shape[dim] - width, cells.shape[dim], axis=dim)
        cells = jnp.concatenate(
            [
                lax.ppermute(tail, axis, [(i, (i + 1) % count) for i in range(ends)]),
                cells,
                lax.ppermute(head, axis, [((i + 1) % count, i) for i in range(ends)]),
            ],
            axis=dim,
        )
    return cells


def normalize(values, along_axis, gain_rows, shift_rows):
    average = jnp.mean(values, axis=along_axis, keepdims=True)
    centered = values - average
    variance = jnp.mean(centered * centered, axis=along_axis, keepdims=True)
    return centered * lax.rsqrt(variance + 1e-05) * gain_rows + shift_rows


def update_hubs(hub_sum, hub_old, weight, bias_row, gain_row, shift_row, q_local, model_width):
    count = hub_sum.shape[0]
    inputs_now = hub_sum.astype(jnp.bfloat16).reshape(count, q_local, model_width)
    linear = (
        jnp.einsum("hqd,de->hqe", inputs_now, weight, preferred_element_type=jnp.float32)
        + bias_row[None, None, :]
    )
    normed = normalize(linear, 2, gain_row[None, None, :], shift_row[None, None, :])
    updated = jax.nn.relu(normed) + hub_old.astype(jnp.float32).reshape(count, q_local, model_width)
    return updated.astype(jnp.bfloat16).reshape(count, q_local * model_width)


def body(
    ent_feat,
    query_head,
    query_rel,
    query_table,
    rel_table,
    layer_weight,
    layer_bias,
    norm_gain,
    norm_shift,
    reg_blocks,
    reg_rel,
    reg_mask,
    hin_blocks,
    hin_rel,
    hin_mask,
    hout_blocks,
    hout_rel,
    hout_mask,
    read_weight,
    read_bias,
    read_out,
):
    ent_devices = lax.axis_size("ent")
    queries = query_head.shape[0]
    q_local = queries // lax.axis_size("qry")
    model_width = ent_feat.shape[0]
    ent_local = ent_feat.shape[1]
    block_size = reg_mask.shape[1]
    blocks_local = ent_local // block_size
    hub_total = HUB_DEV * ent_devices
    hub_block_count = hub_total // block_size
    state_rows = q_local * model_width
    first_block = lax.axis_index("ent") * blocks_local
    first_entity = lax.axis_index("ent") * ent_local
    query_first = lax.axis_index("qry") * q_local
    highest = lax.Precision.HIGHEST
    rel_iota = jnp.arange(query_table.shape[0], dtype=jnp.int32)
    query_onehot = (query_rel[:, None] == rel_iota[None, :]).astype(jnp.bfloat16)
    query_all = jnp.dot(query_onehot, query_table, preferred_element_type=jnp.float32)
    query_local = lax.dynamic_slice_in_dim(query_all, query_first, q_local, 0)
    heads_local = lax.dynamic_slice_in_dim(query_head, query_first, q_local, 0)
    positions = first_entity + jnp.arange(ent_local, dtype=jnp.int32)
    head_hits = (heads_local[:, None] == positions[None, :]).astype(jnp.float32)
    boundary = query_local[:, :, None] * head_hits[:, None, :]
    states = (ent_feat.astype(jnp.float32)[None] + boundary).astype(jnp.bfloat16)
    reg_masks = reg_mask.astype(jnp.bfloat16)
    hin_masks = hin_mask.astype(jnp.bfloat16)
    hout_masks = hout_mask.astype(jnp.bfloat16)
    local_iota = jnp.arange(blocks_local, dtype=jnp.int32)[None, :]
    reg_onehot = (reg_blocks[:, 0][:, None] - first_block == local_iota).astype(jnp.float32)
    reg_sources = reg_blocks[:, 1] - first_block + blocks_local
    hout_onehot = (hout_blocks[:, 0][:, None] - first_block == local_iota).astype(jnp.float32)
    hout_sources = hout_blocks[:, 1]
    hin_onehot = (
        hin_blocks[:, 0][:, None] == jnp.arange(hub_block_count, dtype=jnp.int32)[None, :]
    ).astype(jnp.float32)
    hin_sources = hin_blocks[:, 1] - first_block

    def tile_coefficients(rel_ids, rel_layer):
        rel_onehot = (rel_ids[:, None] == rel_iota[None, :]).astype(jnp.bfloat16)
        rel_rows = jnp.dot(rel_onehot, rel_layer, preferred_element_type=jnp.float32)
        return (query_local[:, :, None] * rel_rows.T[None, :, :]).reshape(state_rows, -1)

    hub_own = jnp.zeros((HUB_DEV, state_rows), jnp.bfloat16)
    for layer_at in range(LAYERS):
        weight = layer_weight[layer_at]
        rel_layer = rel_table[layer_at]
        flat_states = states.reshape(state_rows, ent_local)
        window = padded(flat_states, (("ent", 1),), ent_local)
        window_blocks = window.reshape(state_rows, 3 * blocks_local, block_size)
        gathered = jnp.take(window_blocks, reg_sources, axis=1)
        product = jnp.einsum(
            "ctj,tjk->ctk", gathered, reg_masks, preferred_element_type=jnp.float32
        )
        product = product * tile_coefficients(reg_rel, rel_layer)[:, :, None]
        totals = jnp.einsum("ctk,tb->cbk", product, reg_onehot, precision=highest)
        if layer_at > 0:
            hub_full = lax.all_gather(hub_own, "ent", axis=0, tiled=True)
        else:
            hub_full = jnp.zeros((hub_total, state_rows), jnp.bfloat16)
        hub_view = hub_full.reshape(hub_block_count, block_size, state_rows)
        hub_sources = jnp.take(hub_view, hout_sources, axis=0)
        product = jnp.einsum(
            "tjc,tjk->ctk", hub_sources, hout_masks, preferred_element_type=jnp.float32
        )
        product = product * tile_coefficients(hout_rel, rel_layer)[:, :, None]
        totals = totals + jnp.einsum("ctk,tb->cbk", product, hout_onehot, precision=highest)
        own_blocks = flat_states.reshape(state_rows, blocks_local, block_size)
        hin_gathered = jnp.take(own_blocks, hin_sources, axis=1)
        hin_product = jnp.einsum(
            "ctj,tjk->tkc", hin_gathered, hin_masks, preferred_element_type=jnp.float32
        )
        hin_product = hin_product * tile_coefficients(hin_rel, rel_layer).T[:, None, :]
        partial_value = jnp.einsum(
            "tkc,th->hkc", hin_product, hin_onehot, precision=highest
        ).reshape(hub_total, state_rows)
        inputs_now = (totals.reshape(q_local, model_width, ent_local) + boundary).astype(
            jnp.bfloat16
        )
        linear = (
            jnp.einsum("qdv,de->qev", inputs_now, weight, preferred_element_type=jnp.float32)
            + layer_bias[layer_at][None, :, None]
        )
        normed = normalize(
            linear, 1, norm_gain[layer_at][None, :, None], norm_shift[layer_at][None, :, None]
        )
        states = (jax.nn.relu(normed) + states.astype(jnp.float32)).astype(jnp.bfloat16)
        hub_sum = lax.psum_scatter(partial_value, "ent", scatter_dimension=0, tiled=True)
        hub_own = update_hubs(
            hub_sum,
            hub_own,
            weight,
            layer_bias[layer_at],
            norm_gain[layer_at],
            norm_shift[layer_at],
            q_local,
            model_width,
        )
    read_states = read_weight[:model_width]
    query_part_all = (
        jnp.dot(
            query_all.astype(jnp.bfloat16),
            read_weight[model_width:],
            preferred_element_type=jnp.float32,
        )
        + read_bias[None, :]
    )
    query_part_local = lax.dynamic_slice_in_dim(query_part_all, query_first, q_local, 0)
    moved_states = lax.all_to_all(states, "qry", split_axis=2, concat_axis=0, tiled=True)
    features = jax.nn.relu(
        jnp.einsum("qdv,de->qev", moved_states, read_states, preferred_element_type=jnp.float32)
        + query_part_all[:, :, None]
    )
    scores = jnp.einsum("qev,e->qv", features, read_out, precision=highest)
    hub_view_own = hub_own.reshape(HUB_DEV, q_local, model_width)
    hub_features = jax.nn.relu(
        jnp.einsum("hqd,de->hqe", hub_view_own, read_states, preferred_element_type=jnp.float32)
        + query_part_local[None]
    )
    hub_scores = jnp.einsum("hqe,e->qh", hub_features, read_out, precision=highest)
    return (scores, hub_scores)


def solution(mesh):
    return jax.shard_map(
        body,
        mesh=mesh,
        in_specs=(
            P(None, "ent"),
            P(),
            P(),
            P(),
            P(),
            P(),
            P(),
            P(),
            P(),
            P("ent", None),
            P("ent"),
            P("ent", None, None),
            P("ent", None),
            P("ent"),
            P("ent", None, None),
            P("ent", None),
            P("ent"),
            P("ent", None, None),
            P(),
            P(),
            P(),
        ),
        out_specs=(P(None, ("ent", "qry")), P("qry", "ent")),
        check_vma=False,
    )
```

profile of v0, /device:TPU:0, one launch (start us, length us, event | category | flops | bytes accessed | tf_op | source)
XLA Modules:
  0.0 461.3 jit_solution(1653198230750983543)
XLA Ops:
  13.4 6.3 %collective-permute-start = (bf16[256,1024]{1,0:T(8,128)(2,1)}, bf16[256,1024]{1,0:T(8,128)(2,1)}, u32[]{:S(2)}, u32[]{:S(2)}) collective-permute-start(bf16[256,1024]{1,0:T(8,128)(2,1)} %fusion.90), channel_id=1, source_target_pairs={{0,4},{4,8},{8,12},{12,16},{16,20},{20,24},{24,28},{1,5},{5,9},{9,... | collective-permute-start | bytes 1572872 | tf_op jit(solution)/shard_map/ppermute | solution.py:18
  37.9 4.0 multiply_bitcast_fusion.2
  56.1 3.9 fusion.28
  64.0 48.3 %reduce-scatter.4.cloned.1.call-done = f32[16,256]{1,0:T(8,128)} async-done(((f32[128,256]{1,0:T(8,128)}), f32[16,256]{1,0:T(8,128)}) %reduce-scatter.4.cloned.1.call-update) | async-done | bytes 16400 | tf_op jit(solution)/shard_map/reduce_scatter | solution.py:154
  117.5 5.9 %gather_fusion = bf16[80,256,128]{2,1,0:T(8,128)(2,1)} fusion(bf16[256,24,128]{2,0,1:T(8,128)(2,1)S(1)} %copy.179, s32[1024]{0:T(1024)} %pad_clamp_fusion.1), kind=kCustom, calls=%fused_computation.clone | custom fusion | bytes 10486080 | tf_op jit(solution)/shard_map/jit(_take)/gather | solution.py:117
  123.5 6.6 %bitcast_multiply_fusion.2 = f32[256,80,128]{2,0,1:T(8,128)S(1)} fusion(f32[256,80]{0,1:T(8,128)S(1)} %copy-done.19, bf16[80,256,128]{2,1,0:T(8,128)(2,1)} %gather_fusion, pred[80]{0:T(512)(128)(4,1)S(1)} %copy-done.37, s32[80,128,128]{2,1,0:T(8,128)} %param.38), kind=kOutput, calls=%fused_computation.8 | convolution fusion | flops 677642240 | bytes 21053520 | tf_op jit(solution)/shard_map/ctj,tjk->ctk/dot_general | solution.py:118
  130.1 9.4 %fusion.78 = bf16[256,8,128]{2,1,0:T(8,128)(2,1)S(1)} fusion(f32[256,8,128]{2,1,0:T(8,128)S(1)} %get-tuple-element.12, f32[8,256,128]{2,0,1:T(8,128)S(1)} %copy-done.15, f32[256,80,128]{2,0,1:T(8,128)S(1)} %bitcast_multiply_fusion.2, s32[80]{0:T(128)S(1)} %copy-done.43), kind=kOutput, calls=%fused_computation.76 | convolution fusion | flops 252445312 | bytes 13107520 | tf_op jit(solution)/shard_map/ctk,tb->cbk/dot_general | solution.py:122
  145.9 4.4 multiply_bitcast_fusion.1
  162.6 5.4 %collective-permute-start.2 = (bf16[256,1024]{0,1:T(8,128)(2,1)}, bf16[256,1024]{0,1:T(8,128)(2,1)}, u32[]{:S(2)}, u32[]{:S(2)}) collective-permute-start(bf16[256,1024]{0,1:T(8,128)(2,1)} %copy.184), channel_id=1, source_target_pairs={{0,4},{4,8},{8,12},{12,16},{16,20},{20,24},{24,28},{1,5},{5,9},{9,... | collective-permute-start | bytes 1572872 | tf_op jit(solution)/shard_map/ppermute | solution.py:18
  168.0 52.6 %reduce-scatter.6.cloned.1.call-done = f32[16,256]{1,0:T(8,128)} async-done(((f32[128,256]{1,0:T(8,128)}), f32[16,256]{1,0:T(8,128)}) %reduce-scatter.6.cloned.1.call-update) | async-done | bytes 16400 | tf_op jit(solution)/shard_map/reduce_scatter | solution.py:154
  226.0 32.4 %all_gather.6 = bf16[128,256]{1,0:T(8,128)(2,1)} all-gather(bf16[16,256]{1,0:T(8,128)(2,1)S(1)} %reshape.378), channel_id=1, replica_groups=mesh['ent'=8,'qry'=4] {'ent'}, dimensions={0}, use_global_device_ids=true | all-gather | bytes 73728 | tf_op jit(solution)/shard_map/all_gather | solution.py:124
  260.7 32.4 %all_gather.7 = bf16[128,256]{1,0:T(8,128)(2,1)} all-gather(bf16[16,256]{1,0:T(8,128)(2,1)S(1)} %reshape.382), channel_id=1, replica_groups=mesh['ent'=8,'qry'=4] {'ent'}, dimensions={0}, use_global_device_ids=true | all-gather | bytes 73728 | tf_op jit(solution)/shard_map/all_gather | solution.py:124
  296.5 3.8 fusion.26
  308.3 5.9 %gather_fusion.1 = bf16[80,256,128]{2,1,0:T(8,128)(2,1)} fusion(bf16[256,24,128]{2,0,1:T(8,128)(2,1)S(1)} %pad_maximum_fusion.1, s32[1024]{0:T(1024)} %pad_clamp_fusion.1), kind=kCustom, calls=%fused_computation.2.clone | custom fusion | bytes 10486080 | tf_op jit(solution)/shard_map/jit(_take)/gather | solution.py:117
  314.2 6.5 %bitcast_multiply_fusion.1 = f32[256,80,128]{2,0,1:T(8,128)S(1)} fusion(f32[256,80]{0,1:T(8,128)S(1)} %copy-done.18, bf16[80,256,128]{2,1,0:T(8,128)(2,1)} %gather_fusion.1, pred[80]{0:T(512)(128)(4,1)S(1)} %copy-done.38, s32[80,128,128]{2,1,0:T(8,128)} %param.38), kind=kOutput, calls=%fused_computation.7 | convolution fusion | flops 677642240 | bytes 21053520 | tf_op jit(solution)/shard_map/ctj,tjk->ctk/dot_general | solution.py:118
  320.8 9.4 %fusion.81 = bf16[256,8,128]{2,1,0:T(8,128)(2,1)S(1)} fusion(f32[256,8,128]{2,1,0:T(8,128)S(1)} %get-tuple-element.12, f32[8,256,128]{2,0,1:T(8,128)S(1)} %copy-done.17, f32[256,80,128]{2,0,1:T(8,128)S(1)} %bitcast_multiply_fusion.1, s32[80]{0:T(128)S(1)} %copy-done.44), kind=kOutput, calls=%fused_computation.77 | convolution fusion | flops 252445312 | bytes 13107520 | tf_op jit(solution)/shard_map/ctk,tb->cbk/dot_general | solution.py:122
  336.2 4.2 multiply_bitcast_fusion
  347.8 5.7 %fusion.24 = f32[8,256,128]{2,0,1:T(8,128)} fusion(f32[256,24,128]{2,0,1:T(8,128)} %bitcast_multiply_fusion.3, s32[24]{0:T(128)S(1)} %copy-done.48), kind=kOutput, calls=%fused_computation.30 | convolution fusion | flops 75497664 | bytes 4194400 | tf_op jit(solution)/shard_map/ctk,tb->cbk/dot_general | solution.py:133
  355.0 4.6 collective-permute-start.4
  359.6 49.5 %reduce-scatter.8.cloned.1.call-done = f32[16,256]{1,0:T(8,128)} async-done(((f32[128,256]{1,0:T(8,128)}), f32[16,256]{1,0:T(8,128)}) %reduce-scatter.8.cloned.1.call-update) | async-done | bytes 16400 | tf_op jit(solution)/shard_map/reduce_scatter | solution.py:154
  413.7 5.8 %gather_fusion.3 = bf16[80,256,128]{2,1,0:T(8,128)(2,1)} fusion(bf16[256,24,128]{2,0,1:T(8,128)(2,1)S(1)} %pad_maximum_fusion.2, s32[1024]{0:T(1024)} %pad_clamp_fusion.1), kind=kCustom, calls=%fused_computation.3.clone | custom fusion | bytes 10486080 | tf_op jit(solution)/shard_map/jit(_take)/gather | solution.py:117
  419.5 6.6 %bitcast_multiply_fusion = f32[256,80,128]{2,0,1:T(8,128)S(1)} fusion(f32[256,80]{0,1:T(8,128)S(1)} %copy.203, bf16[80,256,128]{2,1,0:T(8,128)(2,1)} %gather_fusion.3, pred[80]{0:T(512)(128)(4,1)S(1)} %copy-done.38, s32[80,128,128]{2,1,0:T(8,128)} %param.38), kind=kOutput, calls=%fused_computation.6 | convolution fusion | flops 677642240 | bytes 21053520 | tf_op jit(solution)/shard_map/ctj,tjk->ctk/dot_general | solution.py:118
  426.1 9.4 %fusion.84 = bf16[256,8,128]{2,1,0:T(8,128)(2,1)S(1)} fusion(f32[256,8,128]{2,1,0:T(8,128)S(1)} %get-tuple-element.12, f32[8,256,128]{2,0,1:T(8,128)S(1)} %copy-done.16, f32[256,80,128]{2,0,1:T(8,128)S(1)} %bitcast_multiply_fusion, s32[80]{0:T(128)S(1)} %copy-done.45), kind=kOutput, calls=%fused_computation.78 | convolution fusion | flops 252445312 | bytes 13107520 | tf_op jit(solution)/shard_map/ctk,tb->cbk/dot_general | solution.py:122
  443.9 7.6 %all-to-all-done = bf16[4,2,32768]{2,1,0:T(2,128)(2,1)S(1)} async-done(((bf16[4,2,32768]{2,1,0:T(2,128)(2,1)}), bf16[4,2,32768]{2,1,0:T(2,128)(2,1)S(1)}, u32[]{:S(2)}, u32[]{:S(2)}) %all-to-all-start) | async-done | bytes 524320 | tf_op jit(solution)/shard_map/all_to_all | solution.py:175
  (278 shorter events, 115.4 us)
Async XLA Ops:
  7.2 105.1 %reduce-scatter.4.cloned.1.call-start = ((), (), s32[]{:S(2)}) async-start(), calls=%async_computation.4 | async-start | bytes 147456 | tf_op jit(solution)/shard_map/reduce_scatter | solution.py:154
  12.1 102.5 %collective-permute-start.1 = (bf16[256,1024]{1,0:T(8,128)(2,1)}, bf16[256,1024]{1,0:T(8,128)(2,1)}, u32[]{:S(2)}, u32[]{:S(2)}) collective-permute-start(bf16[256,1024]{1,0:T(8,128)(2,1)} %fusion.90), channel_id=1, source_target_pairs={{4,0},{8,4},{12,8},{16,12},{20,16},{24,20},{28,24},{5,1},{9,5},{13... | collective-permute-start | bytes 1572872 | tf_op jit(solution)/shard_map/ppermute | solution.py:20
  13.4 102.4 %collective-permute-start = (bf16[256,1024]{1,0:T(8,128)(2,1)}, bf16[256,1024]{1,0:T(8,128)(2,1)}, u32[]{:S(2)}, u32[]{:S(2)}) collective-permute-start(bf16[256,1024]{1,0:T(8,128)(2,1)} %fusion.90), channel_id=1, source_target_pairs={{0,4},{4,8},{8,12},{12,16},{16,20},{20,24},{24,28},{1,5},{5,9},{9,... | collective-permute-start | bytes 1572872 | tf_op jit(solution)/shard_map/ppermute | solution.py:18
  45.5 8.8 %copy-start.61 = (s32[80,2]{0,1:T(2,128)S(1)}, s32[80,2]{0,1:T(2,128)}, u32[]{:S(2)}) copy-start(s32[80,2]{0,1:T(2,128)} %param.36) | copy-start | bytes 1924
  45.5 9.2 %copy-start.4 = (s32[24,128,128]{2,1,0:T(8,128)S(1)}, s32[24,128,128]{2,1,0:T(8,128)}, u32[]{:S(2)}) copy-start(s32[24,128,128]{2,1,0:T(8,128)} %param.44) | copy-start | bytes 4718596
  49.4 171.2 %reduce-scatter.6.cloned.1.call-start = ((), (), s32[]{:S(2)}) async-start(), calls=%async_computation.5 | async-start | bytes 147456 | tf_op jit(solution)/shard_map/reduce_scatter | solution.py:154
  50.2 9.7 %copy-start.46 = (s32[24]{0:T(128)}, s32[24]{0:T(128)S(1)}, u32[]{:S(2)}) copy-start(s32[24]{0:T(128)S(1)} %subtract_bitcast_fusion) | copy-start | bytes 292
  54.3 58.8 %copy-start.50 = (f32[64]{0:T(128)}, f32[64]{0:T(128)S(1)}, u32[]{:S(2)}) copy-start(f32[64]{0:T(128)S(1)} %get-tuple-element.22) | copy-start | bytes 772
  56.0 60.8 %copy-start.14 = (bf16[256,8,128]{2,1,0:T(8,128)(2,1)S(1)}, bf16[256,8,128]{2,1,0:T(8,128)(2,1)}, u32[]{:S(2)}) copy-start(bf16[256,8,128]{2,1,0:T(8,128)(2,1)} %copy-done.13) | copy-start | bytes 1572868
  60.7 51.6 %copy-start.29 = (f32[16,64]{1,0:T(8,128)}, f32[16,64]{1,0:T(8,128)S(1)}, u32[]{:S(2)}) copy-start(f32[16,64]{1,0:T(8,128)S(1)} %convolution_add_fusion.8) | copy-start | bytes 12292
  130.1 9.6 %copy-start.51 = (f32[64]{0:T(128)S(1)}, f32[64]{0:T(128)}, u32[]{:S(2)}) copy-start(f32[64]{0:T(128)} %copy-done.50) | copy-start | bytes 772
  153.9 140.8 %copy-start.5 = (s32[24,128,128]{2,1,0:T(8,128)S(1)}, s32[24,128,128]{2,1,0:T(8,128)}, u32[]{:S(2)}) copy-start(s32[24,128,128]{2,1,0:T(8,128)} %param.44) | copy-start | bytes 4718596
  157.8 251.2 %reduce-scatter.8.cloned.1.call-start = ((), (), s32[]{:S(2)}) async-start(), calls=%async_computation.6 | async-start | bytes 147456 | tf_op jit(solution)/shard_map/reduce_scatter | solution.py:154
  161.3 141.4 %collective-permute-start.3 = (bf16[256,1024]{0,1:T(8,128)(2,1)}, bf16[256,1024]{0,1:T(8,128)(2,1)}, u32[]{:S(2)}, u32[]{:S(2)}) collective-permute-start(bf16[256,1024]{0,1:T(8,128)(2,1)} %copy.184), channel_id=1, source_target_pairs={{4,0},{8,4},{12,8},{16,12},{20,16},{24,20},{28,24},{5,1},{9,5},{13... | collective-permute-start | bytes 1572872 | tf_op jit(solution)/shard_map/ppermute | solution.py:20
  162.6 142.2 %collective-permute-start.2 = (bf16[256,1024]{0,1:T(8,128)(2,1)}, bf16[256,1024]{0,1:T(8,128)(2,1)}, u32[]{:S(2)}, u32[]{:S(2)}) collective-permute-start(bf16[256,1024]{0,1:T(8,128)(2,1)} %copy.184), channel_id=1, source_target_pairs={{0,4},{4,8},{8,12},{12,16},{16,20},{20,24},{24,28},{1,5},{5,9},{9,... | collective-permute-start | bytes 1572872 | tf_op jit(solution)/shard_map/ppermute | solution.py:18
  225.9 70.6 %copy-start.47 = (s32[24]{0:T(128)S(1)}, s32[24]{0:T(128)}, u32[]{:S(2)}) copy-start(s32[24]{0:T(128)} %copy-done.46) | copy-start | bytes 292
  343.9 9.5 %copy-start.10 = (bf16[4,64,1024]{2,1,0:T(8,128)(2,1)S(1)}, bf16[4,64,1024]{2,1,0:T(8,128)(2,1)}, u32[]{:S(2)}) copy-start(bf16[4,64,1024]{2,1,0:T(8,128)(2,1)} %copy-done.9) | copy-start | bytes 1572868
  347.1 62.8 %copy-start.21 = (bf16[3,64,64]{2,1,0:T(8,128)(2,1)S(1)}, bf16[3,64,64]{2,1,0:T(8,128)(2,1)}, u32[]{:S(2)}) copy-start(bf16[3,64,64]{2,1,0:T(8,128)(2,1)} %param.32) | copy-start | bytes 73732
  347.1 62.8 %copy-start.49 = (f32[64]{0:T(128)S(1)}, f32[64]{0:T(128)}, u32[]{:S(2)}) copy-start(f32[64]{0:T(128)} %get-tuple-element.21) | copy-start | bytes 772
  353.7 56.6 %collective-permute-start.5 = (bf16[256,1024]{0,1:T(8,128)(2,1)S(1)}, bf16[256,1024]{0,1:T(8,128)(2,1)S(1)}, u32[]{:S(2)}, u32[]{:S(2)}) collective-permute-start(bf16[256,1024]{0,1:T(8,128)(2,1)S(1)} %copy.198), channel_id=1, source_target_pairs={{4,0},{8,4},{12,8},{16,12},{20,16},{24,20},{28,24},{5,1},{9,5},{13... | collective-permute-start | bytes 1572872 | tf_op jit(solution)/shard_map/ppermute | solution.py:20
  355.0 56.3 %collective-permute-start.4 = (bf16[256,1024]{0,1:T(8,128)(2,1)S(1)}, bf16[256,1024]{0,1:T(8,128)(2,1)S(1)}, u32[]{:S(2)}, u32[]{:S(2)}) collective-permute-start(bf16[256,1024]{0,1:T(8,128)(2,1)S(1)} %copy.198), channel_id=1, source_target_pairs={{0,4},{4,8},{8,12},{12,16},{16,20},{20,24},{24,28},{1,5},{5,9},{9,... | collective-permute-start | bytes 1572872 | tf_op jit(solution)/shard_map/ppermute | solution.py:18
  437.6 15.1 %copy-start.30 = (f32[16,64]{1,0:T(8,128)S(1)}, f32[16,64]{1,0:T(8,128)}, u32[]{:S(2)}) copy-start(f32[16,64]{1,0:T(8,128)} %copy-done.29) | copy-start | bytes 12292
  439.2 12.3 %all-to-all-start = ((bf16[4,2,32768]{2,1,0:T(2,128)(2,1)}), bf16[4,2,32768]{2,1,0:T(2,128)(2,1)S(1)}, u32[]{:S(2)}, u32[]{:S(2)}) async-start(bf16[4,2,32768]{2,1,0:T(2,128)(2,1)} %reshape.477), calls=%async_computation.2 | async-start | bytes 1048576 | tf_op jit(solution)/shard_map/all_to_all | solution.py:175
  442.7 11.6 %copy-start.1 = (bf16[822,64]{0,1:T(8,128)(2,1)S(1)}, bf16[822,64]{0,1:T(8,128)(2,1)}, u32[]{:S(2)}) copy-start(bf16[822,64]{0,1:T(8,128)(2,1)} %param.30) | copy-start | bytes 315652
  (50 other events, 188.3 us)
Sparse Core Ops, SparseCore 0:
  49.6 62.6 reduce-scatter.3
  158.0 62.5 reduce-scatter.5
  347.9 61.0 reduce-scatter.7
where the time goes:
time: 468 us; the launch traced here: 461 us
  waiting for transfers between devices  158 us (34%)
  matrix products  107 us (23%)
  local copies, waits for them, and re-layouts  71.9 us (15%)
  blocking collectives  64.8 us (14%)
  starting transfers between devices  23.9 us (5%)
  other arithmetic  20.6 us (4%)
  between operations  15.3 us (3%)
    reduce_scatter x3, waiting for transfers between devices, body(): lax.psum_scatter(partial_value, 'ent', scatter_dimension=0, tiled=True)  150 us
    all_gather x2, blocking collectives, body(): hub_full = lax.all_gather(hub_own, 'ent', axis=0, tiled=True)  64.8 us
    dot_general x3, matrix products, body(): totals = jnp.einsum('ctk,tb->cbk', product, reg_onehot, precision=highest)  28.1 us
    dot_general x3, matrix products, body(): jnp.einsum('ctj,tjk->ctk', gathered, reg_masks, preferred_element_type=jn...  19.8 us
    gather x3, local copies, waits for them, and re-layouts, body(): gathered = jnp.take(window_blocks, reg_sources, axis=1)  17.7 us
    ppermute x3, starting transfers between devices, padded(): lax.ppermute(tail, axis, [(i, (i + 1) % count) for i in range(ends)])  16.3 us
    dot_general x3, matrix products, body(): jnp.einsum('ctk,tb->cbk', product, hout_onehot, precision=highest)  13.3 us
    dot_general x3, matrix products, body(): jnp.einsum('ctj,tjk->tkc', hin_gathered, hin_masks, preferred_element_typ...  12.6 us
  transfers between devices with their start and end apart: 10, of which 4 were waited for; matrix products, arithmetic and copies ran while one was open for 17% of the time, Pallas kernels for 0%

commit v1 on v0

--- a/solution.py
+++ b/solution.py
@@ -121,7 +121,18 @@
         product = product * tile_coefficients(reg_rel, rel_layer)[:, :, None]
         totals = jnp.einsum("ctk,tb->cbk", product, reg_onehot, precision=highest)
         if layer_at > 0:
-            hub_full = lax.all_gather(hub_own, "ent", axis=0, tiled=True)
+
+            def wrap_threads(packet):
+                axis_len = lax.axis_size("ent")
+                samples = []
+                for rr in range(packet.ndim):
+                    samples.append(axis_len if rr == 0 else 1)
+                y2 = lax.all_to_all(
+                    jnp.tile(packet, samples), "ent", split_axis=0, tiled=True, concat_axis=0
+                )
+                return y2
+
+            hub_full = wrap_threads(hub_own)
         else:
             hub_full = jnp.zeros((hub_total, state_rows), jnp.bfloat16)
         hub_view = hub_full.reshape(hub_block_count, block_size, state_rows)

time: 468 us -> 436 us (0.932)
  blocking collectives: 64.8 us -> 0 us
  waiting for transfers between devices: 158 us -> 184 us
  starting transfers between devices: 23.9 us -> 32 us
    all_gather x2 -> x0, blocking collectives: 64.8 us -> none  [body(): hub_full = lax.all_gather(hub_own, 'ent', axis=0, tiled=True)]
    reduce_scatter x3, waiting for transfers between devices: 150 us -> 167 us  [body(): lax.psum_scatter(partial_value, 'ent', scatter_dimension=0, tiled=True)]
    all_to_all x0 -> x2, starting transfers between devices: none -> 7.62 us  [wrap_threads(): lax.all_to_all(jnp.tile(packet, samples), 'ent', split_axis=0, tiled=True...]
    all_to_all x0 -> x2, waiting for transfers between devices: none -> 6.09 us  [wrap_threads(): lax.all_to_all(jnp.tile(packet, samples), 'ent', split_axis=0, tiled=True...]
    unnamed x136 -> x134, local copies, waits for them, and re-layouts: 10.7 us -> 10.8 us
  transfers between devices with their start and end apart: 10 -> 12, of which waited for: 4 -> 6; matrix products, arithmetic and copies ran while one was open for 17% -> 17% of each run, Pallas kernels for 0% -> 0%
where the time goes in v1:
time: 436 us; the launch traced here: 429 us
  waiting for transfers between devices  184 us (42%)
  matrix products  104 us (24%)
  local copies, waits for them, and re-layouts  73.6 us (17%)
  starting transfers between devices  32 us (7%)
  other arithmetic  20.2 us (5%)
  between operations  15.2 us (3%)
    reduce_scatter x3, waiting for transfers between devices, body(): lax.psum_scatter(partial_value, 'ent', scatter_dimension=0, tiled=True)  167 us
    dot_general x3, matrix products, body(): totals = jnp.einsum('ctk,tb->cbk', product, reg_onehot, precision=highest)  28.1 us
    dot_general x3, matrix products, body(): jnp.einsum('ctj,tjk->ctk', gathered, reg_masks, preferred_element_type=jn...  19.8 us
    gather x3, local copies, waits for them, and re-layouts, body(): gathered = jnp.take(window_blocks, reg_sources, axis=1)  17.5 us
    ppermute x3, starting transfers between devices, padded(): lax.ppermute(tail, axis, [(i, (i + 1) % count) for i in range(ends)])  16.7 us
    dot_general x3, matrix products, body(): jnp.einsum('ctk,tb->cbk', product, hout_onehot, precision=highest)  13.4 us
    dot_general x3, matrix products, body(): jnp.einsum('ctj,tjk->tkc', hin_gathered, hin_masks, preferred_element_typ...  12.7 us
    unnamed x134, local copies, waits for them, and re-layouts  10.8 us
  transfers between devices with their start and end apart: 12, of which 6 were waited for; matrix products, arithmetic and copies ran while one was open for 17% of the time, Pallas kernels for 0%

profile of v1, /device:TPU:0, one launch (start us, length us, event | category | flops | bytes accessed | tf_op | source)
XLA Modules:
  0.0 429.4 jit_solution(3800619592863717761)
XLA Ops:
  13.4 6.3 %collective-permute-start = (bf16[256,1024]{1,0:T(8,128)(2,1)}, bf16[256,1024]{1,0:T(8,128)(2,1)}, u32[]{:S(2)}, u32[]{:S(2)}) collective-permute-start(bf16[256,1024]{1,0:T(8,128)(2,1)} %fusion.90), channel_id=1, source_target_pairs={{0,4},{4,8},{8,12},{12,16},{16,20},{20,24},{24,28},{1,5},{5,9},{9,... | collective-permute-start | bytes 1572872 | tf_op jit(solution)/shard_map/ppermute | solution.py:18
  38.0 4.0 multiply_bitcast_fusion.2
  54.5 3.9 fusion.28
  60.1 52.3 %reduce-scatter.4.cloned.1.call-done = f32[16,256]{1,0:T(8,128)} async-done(((f32[128,256]{1,0:T(8,128)}), f32[16,256]{1,0:T(8,128)}) %reduce-scatter.4.cloned.1.call-update) | async-done | bytes 16400 | tf_op jit(solution)/shard_map/reduce_scatter | solution.py:165
  117.6 5.8 %gather_fusion = bf16[80,256,128]{2,1,0:T(8,128)(2,1)} fusion(bf16[256,24,128]{2,0,1:T(8,128)(2,1)S(1)} %copy.179, s32[1024]{0:T(1024)} %pad_clamp_fusion.1), kind=kCustom, calls=%fused_computation.clone | custom fusion | bytes 10486080 | tf_op jit(solution)/shard_map/jit(_take)/gather | solution.py:117
  123.4 6.6 %bitcast_multiply_fusion.2 = f32[256,80,128]{2,0,1:T(8,128)S(1)} fusion(f32[256,80]{0,1:T(8,128)S(1)} %copy.180, bf16[80,256,128]{2,1,0:T(8,128)(2,1)} %gather_fusion, pred[80]{0:T(512)(128)(4,1)S(1)} %copy-done.39, s32[80,128,128]{2,1,0:T(8,128)} %param.38), kind=kOutput, calls=%fused_computation.8 | convolution fusion | flops 677642240 | bytes 21053520 | tf_op jit(solution)/shard_map/ctj,tjk->ctk/dot_general | solution.py:118
  130.1 9.4 %fusion.78 = bf16[256,8,128]{2,1,0:T(8,128)(2,1)S(1)} fusion(f32[256,8,128]{2,1,0:T(8,128)S(1)} %get-tuple-element.12, f32[8,256,128]{2,0,1:T(8,128)S(1)} %copy-done.16, f32[256,80,128]{2,0,1:T(8,128)S(1)} %bitcast_multiply_fusion.2, s32[80]{0:T(128)S(1)} %copy-done.42), kind=kOutput, calls=%fused_computation.76 | convolution fusion | flops 252445312 | bytes 13107520 | tf_op jit(solution)/shard_map/ctk,tb->cbk/dot_general | solution.py:122
  145.1 4.5 %multiply_bitcast_fusion.1 = f32[24,128,256]{1,2,0:T(8,128)} fusion(bf16[24,256,128]{2,1,0:T(8,128)(2,1)} %gather_fusion.4, f32[24,256]{1,0:T(8,128)} %get-tuple-element.27, pred[24]{0:T(512)(128)(4,1)S(1)} %copy-done.37, s32[24,128,128]{2,1,0:T(8,128)S(1)} %copy-done.7), kind=kOutput, calls=%fused_computation.37 | convolution fusion | flops 203292672 | bytes 6316056 | tf_op jit(solution)/shard_map/ctj,tjk->tkc/dot_general | solution.py:147
  157.9 60.3 %reduce-scatter.6.cloned.1.call-done = f32[16,256]{1,0:T(8,128)} async-done(((f32[128,256]{1,0:T(8,128)}), f32[16,256]{1,0:T(8,128)}) %reduce-scatter.6.cloned.1.call-update) | async-done | bytes 16400 | tf_op jit(solution)/shard_map/reduce_scatter | solution.py:165
  227.3 6.1 %all-to-all-done = bf16[8,16,256]{2,1,0:T(8,128)(2,1)S(1)} async-done(((bf16[8,16,256]{2,1,0:T(8,128)(2,1)}), bf16[8,16,256]{2,1,0:T(8,128)(2,1)S(1)}, u32[]{:S(2)}, u32[]{:S(2)}) %all-to-all-start) | async-done | bytes 65568 | tf_op jit(solution)/shard_map/all_to_all | solution.py:130
  234.0 4.0 all-to-all-start.1
  245.5 5.3 %collective-permute-start.2 = (bf16[256,1024]{0,1:T(8,128)(2,1)}, bf16[256,1024]{0,1:T(8,128)(2,1)}, u32[]{:S(2)}, u32[]{:S(2)}) collective-permute-start(bf16[256,1024]{0,1:T(8,128)(2,1)} %copy.184), channel_id=1, source_target_pairs={{0,4},{4,8},{8,12},{12,16},{16,20},{20,24},{24,28},{1,5},{5,9},{9,... | collective-permute-start | bytes 1572872 | tf_op jit(solution)/shard_map/ppermute | solution.py:18
  264.1 3.8 collective-permute-done.2
  271.4 5.9 %gather_fusion.1 = bf16[80,256,128]{2,1,0:T(8,128)(2,1)} fusion(bf16[256,24,128]{2,0,1:T(8,128)(2,1)S(1)} %pad_maximum_fusion.1, s32[1024]{0:T(1024)} %pad_clamp_fusion.1), kind=kCustom, calls=%fused_computation.2.clone | custom fusion | bytes 10486080 | tf_op jit(solution)/shard_map/jit(_take)/gather | solution.py:117
  277.4 6.5 %bitcast_multiply_fusion.1 = f32[256,80,128]{2,0,1:T(8,128)S(1)} fusion(f32[256,80]{0,1:T(8,128)S(1)} %copy-done.18, bf16[80,256,128]{2,1,0:T(8,128)(2,1)} %gather_fusion.1, pred[80]{0:T(512)(128)(4,1)S(1)} %copy-done.40, s32[80,128,128]{2,1,0:T(8,128)} %param.38), kind=kOutput, calls=%fused_computation.7 | convolution fusion | flops 677642240 | bytes 21053520 | tf_op jit(solution)/shard_map/ctj,tjk->ctk/dot_general | solution.py:118
  283.9 9.4 %fusion.81 = bf16[256,8,128]{2,1,0:T(8,128)(2,1)S(1)} fusion(f32[256,8,128]{2,1,0:T(8,128)S(1)} %get-tuple-element.12, f32[8,256,128]{2,0,1:T(8,128)S(1)} %copy-done.17, f32[256,80,128]{2,0,1:T(8,128)S(1)} %bitcast_multiply_fusion.1, s32[80]{0:T(128)S(1)} %copy-done.43), kind=kOutput, calls=%fused_computation.77 | convolution fusion | flops 252445312 | bytes 13107520 | tf_op jit(solution)/shard_map/ctk,tb->cbk/dot_general | solution.py:122
  299.3 4.2 multiply_bitcast_fusion
  310.9 5.7 %fusion.24 = f32[8,256,128]{2,0,1:T(8,128)} fusion(f32[256,24,128]{2,0,1:T(8,128)} %bitcast_multiply_fusion.3, s32[24]{0:T(128)S(1)} %copy-done.47), kind=kOutput, calls=%fused_computation.30 | convolution fusion | flops 75497664 | bytes 4194400 | tf_op jit(solution)/shard_map/ctk,tb->cbk/dot_general | solution.py:144
  318.1 5.1 %collective-permute-start.4 = (bf16[256,1024]{0,1:T(8,128)(2,1)S(1)}, bf16[256,1024]{0,1:T(8,128)(2,1)S(1)}, u32[]{:S(2)}, u32[]{:S(2)}) collective-permute-start(bf16[256,1024]{0,1:T(8,128)(2,1)S(1)} %copy.198), channel_id=1, source_target_pairs={{0,4},{4,8},{8,12},{12,16},{16,20},{20,24},{24,28},{1,5},{5,9},{9,... | collective-permute-start | bytes 1572872 | tf_op jit(solution)/shard_map/ppermute | solution.py:18
  323.2 54.0 %reduce-scatter.8.cloned.1.call-done = f32[16,256]{1,0:T(8,128)} async-done(((f32[128,256]{1,0:T(8,128)}), f32[16,256]{1,0:T(8,128)}) %reduce-scatter.8.cloned.1.call-update) | async-done | bytes 16400 | tf_op jit(solution)/shard_map/reduce_scatter | solution.py:165
  381.8 5.8 %gather_fusion.3 = bf16[80,256,128]{2,1,0:T(8,128)(2,1)} fusion(bf16[256,24,128]{2,0,1:T(8,128)(2,1)S(1)} %pad_maximum_fusion.2, s32[1024]{0:T(1024)} %pad_clamp_fusion.1), kind=kCustom, calls=%fused_computation.3.clone | custom fusion | bytes 10486080 | tf_op jit(solution)/shard_map/jit(_take)/gather | solution.py:117
  387.6 6.6 %bitcast_multiply_fusion = f32[256,80,128]{2,0,1:T(8,128)S(1)} fusion(f32[256,80]{0,1:T(8,128)S(1)} %copy.203, bf16[80,256,128]{2,1,0:T(8,128)(2,1)} %gather_fusion.3, pred[80]{0:T(512)(128)(4,1)S(1)} %copy-done.40, s32[80,128,128]{2,1,0:T(8,128)} %param.38), kind=kOutput, calls=%fused_computation.6 | convolution fusion | flops 677642240 | bytes 21053520 | tf_op jit(solution)/shard_map/ctj,tjk->ctk/dot_general | solution.py:118
  394.3 9.4 %fusion.84 = bf16[256,8,128]{2,1,0:T(8,128)(2,1)S(1)} fusion(f32[256,8,128]{2,1,0:T(8,128)S(1)} %get-tuple-element.12, f32[8,256,128]{2,0,1:T(8,128)S(1)} %copy-done.15, f32[256,80,128]{2,0,1:T(8,128)S(1)} %bitcast_multiply_fusion, s32[80]{0:T(128)S(1)} %copy-done.44), kind=kOutput, calls=%fused_computation.78 | convolution fusion | flops 252445312 | bytes 13107520 | tf_op jit(solution)/shard_map/ctk,tb->cbk/dot_general | solution.py:122
  412.0 7.6 %all-to-all-done.2 = bf16[4,2,32768]{2,1,0:T(2,128)(2,1)S(1)} async-done(((bf16[4,2,32768]{2,1,0:T(2,128)(2,1)}), bf16[4,2,32768]{2,1,0:T(2,128)(2,1)S(1)}, u32[]{:S(2)}, u32[]{:S(2)}) %all-to-all-start.2) | async-done | bytes 524320 | tf_op jit(solution)/shard_map/all_to_all | solution.py:186
  (280 shorter events, 121.7 us)
Async XLA Ops:
  7.2 105.2 %reduce-scatter.4.cloned.1.call-start = ((), (), s32[]{:S(2)}) async-start(), calls=%async_computation.6 | async-start | bytes 147456 | tf_op jit(solution)/shard_map/reduce_scatter | solution.py:165
  12.1 102.6 %collective-permute-start.1 = (bf16[256,1024]{1,0:T(8,128)(2,1)}, bf16[256,1024]{1,0:T(8,128)(2,1)}, u32[]{:S(2)}, u32[]{:S(2)}) collective-permute-start(bf16[256,1024]{1,0:T(8,128)(2,1)} %fusion.90), channel_id=1, source_target_pairs={{4,0},{8,4},{12,8},{16,12},{20,16},{24,20},{28,24},{5,1},{9,5},{13... | collective-permute-start | bytes 1572872 | tf_op jit(solution)/shard_map/ppermute | solution.py:20
  13.4 102.5 %collective-permute-start = (bf16[256,1024]{1,0:T(8,128)(2,1)}, bf16[256,1024]{1,0:T(8,128)(2,1)}, u32[]{:S(2)}, u32[]{:S(2)}) collective-permute-start(bf16[256,1024]{1,0:T(8,128)(2,1)} %fusion.90), channel_id=1, source_target_pairs={{0,4},{4,8},{8,12},{12,16},{16,20},{20,24},{24,28},{1,5},{5,9},{9,... | collective-permute-start | bytes 1572872 | tf_op jit(solution)/shard_map/ppermute | solution.py:18
  45.6 7.7 %copy-start.4 = (s32[24,128,128]{2,1,0:T(8,128)S(1)}, s32[24,128,128]{2,1,0:T(8,128)}, u32[]{:S(2)}) copy-start(s32[24,128,128]{2,1,0:T(8,128)} %param.44) | copy-start | bytes 4718596
  49.5 168.6 %reduce-scatter.6.cloned.1.call-start = ((), (), s32[]{:S(2)}) async-start(), calls=%async_computation.7 | async-start | bytes 147456 | tf_op jit(solution)/shard_map/reduce_scatter | solution.py:165
  50.4 8.0 %copy-start.45 = (s32[24]{0:T(128)}, s32[24]{0:T(128)S(1)}, u32[]{:S(2)}) copy-start(s32[24]{0:T(128)S(1)} %subtract_bitcast_fusion) | copy-start | bytes 292
  51.8 61.4 %copy-start.49 = (f32[64]{0:T(128)}, f32[64]{0:T(128)S(1)}, u32[]{:S(2)}) copy-start(f32[64]{0:T(128)S(1)} %get-tuple-element.22) | copy-start | bytes 772
  54.5 62.5 %copy-start.14 = (bf16[256,8,128]{2,1,0:T(8,128)(2,1)S(1)}, bf16[256,8,128]{2,1,0:T(8,128)(2,1)}, u32[]{:S(2)}) copy-start(bf16[256,8,128]{2,1,0:T(8,128)(2,1)} %copy-done.13) | copy-start | bytes 1572868
  130.1 9.6 %copy-start.21 = (bf16[3,64,64]{2,1,0:T(8,128)(2,1)S(1)}, bf16[3,64,64]{2,1,0:T(8,128)(2,1)}, u32[]{:S(2)}) copy-start(bf16[3,64,64]{2,1,0:T(8,128)(2,1)} %param.32) | copy-start | bytes 73732
  130.1 9.6 %copy-start.50 = (f32[64]{0:T(128)S(1)}, f32[64]{0:T(128)}, u32[]{:S(2)}) copy-start(f32[64]{0:T(128)} %copy-done.49) | copy-start | bytes 772
  153.2 100.8 %copy-start.5 = (s32[24,128,128]{2,1,0:T(8,128)S(1)}, s32[24,128,128]{2,1,0:T(8,128)}, u32[]{:S(2)}) copy-start(s32[24,128,128]{2,1,0:T(8,128)} %param.44) | copy-start | bytes 4718596
  222.8 10.5 %all-to-all-start = ((bf16[8,16,256]{2,1,0:T(8,128)(2,1)}), bf16[8,16,256]{2,1,0:T(8,128)(2,1)S(1)}, u32[]{:S(2)}, u32[]{:S(2)}) async-start(bf16[8,16,256]{2,1,0:T(8,128)(2,1)} %tile.17), calls=%async_computation.1 | async-start | bytes 131072 | tf_op jit(solution)/shard_map/all_to_all | solution.py:130
  234.0 18.4 %all-to-all-start.1 = ((bf16[8,16,256]{2,1,0:T(8,128)(2,1)}), bf16[8,16,256]{2,1,0:T(8,128)(2,1)}, u32[]{:S(2)}, u32[]{:S(2)}) async-start(bf16[8,16,256]{2,1,0:T(8,128)(2,1)} %tile.19), calls=%async_computation.3 | async-start | bytes 131072 | tf_op jit(solution)/shard_map/all_to_all | solution.py:130
  238.0 139.2 %reduce-scatter.8.cloned.1.call-start = ((), (), s32[]{:S(2)}) async-start(), calls=%async_computation.8 | async-start | bytes 147456 | tf_op jit(solution)/shard_map/reduce_scatter | solution.py:165
  240.6 15.2 %copy-start.46 = (s32[24]{0:T(128)S(1)}, s32[24]{0:T(128)}, u32[]{:S(2)}) copy-start(s32[24]{0:T(128)} %copy-done.45) | copy-start | bytes 292
  244.3 17.9 %collective-permute-start.3 = (bf16[256,1024]{0,1:T(8,128)(2,1)}, bf16[256,1024]{0,1:T(8,128)(2,1)}, u32[]{:S(2)}, u32[]{:S(2)}) collective-permute-start(bf16[256,1024]{0,1:T(8,128)(2,1)} %copy.184), channel_id=1, source_target_pairs={{4,0},{8,4},{12,8},{16,12},{20,16},{24,20},{28,24},{5,1},{9,5},{13... | collective-permute-start | bytes 1572872 | tf_op jit(solution)/shard_map/ppermute | solution.py:20
  245.5 22.4 %collective-permute-start.2 = (bf16[256,1024]{0,1:T(8,128)(2,1)}, bf16[256,1024]{0,1:T(8,128)(2,1)}, u32[]{:S(2)}, u32[]{:S(2)}) collective-permute-start(bf16[256,1024]{0,1:T(8,128)(2,1)} %copy.184), channel_id=1, source_target_pairs={{0,4},{4,8},{8,12},{12,16},{16,20},{20,24},{24,28},{1,5},{5,9},{9,... | collective-permute-start | bytes 1572872 | tf_op jit(solution)/shard_map/ppermute | solution.py:18
  307.0 9.5 %copy-start.10 = (bf16[4,64,1024]{2,1,0:T(8,128)(2,1)S(1)}, bf16[4,64,1024]{2,1,0:T(8,128)(2,1)}, u32[]{:S(2)}) copy-start(bf16[4,64,1024]{2,1,0:T(8,128)(2,1)} %copy-done.9) | copy-start | bytes 1572868
  310.2 67.8 %copy-start.22 = (bf16[3,64,64]{2,1,0:T(8,128)(2,1)S(1)}, bf16[3,64,64]{2,1,0:T(8,128)(2,1)}, u32[]{:S(2)}) copy-start(bf16[3,64,64]{2,1,0:T(8,128)(2,1)} %param.32) | copy-start | bytes 73732
  310.2 67.8 %copy-start.48 = (f32[64]{0:T(128)S(1)}, f32[64]{0:T(128)}, u32[]{:S(2)}) copy-start(f32[64]{0:T(128)} %get-tuple-element.21) | copy-start | bytes 772
  316.8 61.6 %collective-permute-start.5 = (bf16[256,1024]{0,1:T(8,128)(2,1)S(1)}, bf16[256,1024]{0,1:T(8,128)(2,1)S(1)}, u32[]{:S(2)}, u32[]{:S(2)}) collective-permute-start(bf16[256,1024]{0,1:T(8,128)(2,1)S(1)} %copy.198), channel_id=1, source_target_pairs={{4,0},{8,4},{12,8},{16,12},{20,16},{24,20},{28,24},{5,1},{9,5},{13... | collective-permute-start | bytes 1572872 | tf_op jit(solution)/shard_map/ppermute | solution.py:20
  318.1 61.4 %collective-permute-start.4 = (bf16[256,1024]{0,1:T(8,128)(2,1)S(1)}, bf16[256,1024]{0,1:T(8,128)(2,1)S(1)}, u32[]{:S(2)}, u32[]{:S(2)}) collective-permute-start(bf16[256,1024]{0,1:T(8,128)(2,1)S(1)} %copy.198), channel_id=1, source_target_pairs={{0,4},{4,8},{8,12},{12,16},{16,20},{20,24},{24,28},{1,5},{5,9},{9,... | collective-permute-start | bytes 1572872 | tf_op jit(solution)/shard_map/ppermute | solution.py:18
  407.3 12.3 %all-to-all-start.2 = ((bf16[4,2,32768]{2,1,0:T(2,128)(2,1)}), bf16[4,2,32768]{2,1,0:T(2,128)(2,1)S(1)}, u32[]{:S(2)}, u32[]{:S(2)}) async-start(bf16[4,2,32768]{2,1,0:T(2,128)(2,1)} %reshape.487), calls=%async_computation.4 | async-start | bytes 1048576 | tf_op jit(solution)/shard_map/all_to_all | solution.py:186
  410.8 11.6 %copy-start.1 = (bf16[822,64]{0,1:T(8,128)(2,1)S(1)}, bf16[822,64]{0,1:T(8,128)(2,1)}, u32[]{:S(2)}) copy-start(bf16[822,64]{0,1:T(8,128)(2,1)} %param.30) | copy-start | bytes 315652
  (51 other events, 201.3 us)
Sparse Core Ops, SparseCore 0:
  49.6 62.7 reduce-scatter.3
  157.2 60.8 reduce-scatter.5
  311.0 66.0 reduce-scatter.7
